TPU v7x, 256 devices: a whole 4x4x8 slice. The times are simulated.
256 devices in a mesh: grp: 16 (over z, y_lo), blk: 16 (over y_hi, x, core).
Axes of the slice: x: 4, y: 4 (y_hi: 2, y_lo: 2; y = y_hi * 2 + y_lo), z: 8, core: 2. Of those that a mesh axis runs over, the one named last changes fastest.
Arguments:
- states: bfloat16 [524288, 768], P(('grp', 'blk')), may hold values from -6 to 6
- query_weight: bfloat16 [768, 768], replicated, may hold values from -0.21875 to 0.21875
- attempts: bfloat16 [16384, 768], P(('grp', 'blk')), may hold values from -6 to 6
- attempt_theorem: int32 [16384], P('grp'), may hold values from 0 to 15
- positive: int32 [524288], P(('grp', 'blk')), may hold values from 0 to 1023
Outputs:
- loss: float32 [524288], P(('grp', 'blk'))
- grad_attempts: float32 [16384, 768], P(('grp', 'blk'))
- grad_weight: float32 [768, 768], replicated
All inputs are finite; a program needn't handle non-finite values.
Results may differ from a plain program's by a relative error of at most 0.012.
Values may be sent and summed in bfloat16 or wider, within the bound.
No kernel may reach another device: no remote copies, remote signals or barrier semaphores. Data moves between devices by JAX's collectives and lax.ppermute only.
A program may use at most 64 MiB of HBM per device.

v0:
```python
import jax
import jax.numpy as jnp
from jax import lax
from jax.sharding import PartitionSpec as P

logit_sharpness = 0.07
epsilon = 1e-06


def normalized_rows(values):
    return values * lax.rsqrt(jnp.mean(values * values, axis=-1, keepdims=True) + epsilon)


def on_device(states, query_weight, attempts, attempt_theorem, positive):
    vector_dimension = states.shape[1]
    logit_multiplier = 1.0 / (logit_sharpness * vector_dimension)
    attempt_rows_float, attempt_back = jax.vjp(normalized_rows, attempts.astype(jnp.float32))
    candidate_direction = attempt_rows_float.astype(jnp.bfloat16)
    proj = jnp.dot(states, query_weight, preferred_element_type=jnp.float32)
    query_float, query_back = jax.vjp(normalized_rows, proj)
    query_unit = query_float.astype(jnp.bfloat16)
    anchor_lemma_label = jnp.take(attempt_theorem, positive)
    panel = lax.all_gather(candidate_direction, "blk", axis=0, tiled=True)
    scores = (
        lax.dot_general(
            query_unit, panel, (((1,), (1,)), ((), ())), preferred_element_type=jnp.float32
        )
        * logit_multiplier
    )
    mask = anchor_lemma_label[:, None] == attempt_theorem[None, :]
    expo = jnp.where(mask, jnp.exp(scores), 0.0)
    total = jnp.sum(expo, axis=1)
    columns = lax.broadcasted_iota(jnp.int32, scores.shape, 1)
    chosen = columns == positive[:, None]
    pos_score = jnp.sum(jnp.where(chosen, scores, 0.0), axis=1)
    losses = jnp.log(total) - pos_score
    weights = (expo / total[:, None] - chosen.astype(jnp.float32)).astype(jnp.bfloat16)
    grad_qunit = jnp.dot(weights, panel, preferred_element_type=jnp.float32) * logit_multiplier
    grad_aunit = lax.psum_scatter(
        (
            lax.dot_general(
                weights, query_unit, (((0,), (0,)), ((), ())), preferred_element_type=jnp.float32
            )
            * logit_multiplier
        ).astype(jnp.bfloat16),
        "blk",
        scatter_dimension=0,
        tiled=True,
    ).astype(jnp.float32)
    grad_attempts = attempt_back(grad_aunit)[0]
    grad_proj = query_back(grad_qunit)[0].astype(jnp.bfloat16)
    weight_term = lax.dot_general(
        states, grad_proj, (((0,), (0,)), ((), ())), preferred_element_type=jnp.float32
    )
    grad_weight = lax.psum(weight_term, ("grp", "blk"))
    return (losses, grad_attempts, grad_weight)


def solution(mesh):
    in_specs = (P(("grp", "blk"), None), P(), P(("grp", "blk"), None), P("grp"), P(("grp", "blk")))
    out_specs = (P(("grp", "blk")), P(("grp", "blk"), None), P())
    return jax.shard_map(
        on_device, mesh=mesh, in_specs=in_specs, out_specs=out_specs, check_vma=False
    )
```

profile of v0, /device:TPU:2, one launch (start us, length us, event | category | flops | bytes accessed | tf_op | source)
XLA Modules:
  0.0 437.2 jit_solution(6341290176718321154)
XLA Ops:
  7.2 0.0 copy-start
  7.2 0.0 all-gather.2.cloned.1.call-start
  7.2 1.2 fusion.10
  8.4 1.6 fusion.11
  10.0 0.0 all-gather.2.cloned.1.call-update
  10.1 0.0 all-reduce.2.cloned.1.call-start
  10.1 0.7 fusion.14
  10.8 10.2 %gather_fusion = s32[2048]{0:T(1024)S(1)} fusion(s32[1024]{0:T(1024)} %param.8, s32[2048]{0:T(1024)S(1)} %fusion.14), kind=kCustom, calls=%fused_computation | custom fusion | bytes 24576 | tf_op jit(solution)/shard_map/jit(_take)/gather | solution.py:22
  21.0 0.0 copy-done
  21.1 0.0 copy-start.4
  21.1 0.0 copy-start.1
  21.1 5.8 %multiply_reduce_fusion.1 = (f32[2048]{0:T(1024)S(1)}, f32[2048,768]{0,1:T(8,128)}) fusion(bf16[2048,768]{1,0:T(8,128)(2,1)S(1)} %copy-done, bf16[768,768]{1,0:T(8,128)(2,1)} %param.6), kind=kOutput, calls=%fused_computation.10 | convolution fusion | flops 2419062784 | bytes 10625024 | tf_op jit(solution)/shard_map/dot_general | solution.py:19
  26.9 0.0 copy-done.4
  26.9 38.6 %all-gather.2.cloned.1.call-done = bf16[1024,768]{1,0:T(8,128)(2,1)} async-done(((bf16[64,768]{1,0:T(8,128)(2,1)}), bf16[1024,768]{1,0:T(8,128)(2,1)}) %all-gather.2.cloned.1.call-update) | async-done | bytes 1572880 | tf_op jit(solution)/shard_map/all_gather | solution.py:23
  65.5 0.0 copy-done.1
  65.5 8.2 %fusion = (f32[2048]{0:T(1024)S(1)}, f32[2048]{0:T(1024)S(1)}, f32[2048,1024]{0,1:T(8,128)S(1)}) fusion(s32[2048]{0:T(1024)S(1)} %and_select_fusion, s32[1024]{0:T(1024)S(1)} %copy-done.1, s32[2048]{0:T(1024)S(1)} %copy-done.4, bf16[1024,768]{1,0:T(8,128)(2,1)} %all-gather.2.cloned.1.call-done, f32[2048,768]{0,1:T(8,128)} %get-tuple-element.14, ...), kind=kOutput, calls=%fused_computation.6 | convolution fusion | flops 3239047168 | bytes 16297984 | tf_op jit(solution)/shard_map/dot_general | solution.py:25
  73.7 0.0 copy-start.5
  73.7 0.0 copy-start.6
  73.7 3.8 subtract_convert_fusion
  77.6 0.0 copy-done.5
  77.6 0.0 copy-done.6
  77.6 0.0 copy-start.2
  77.6 4.1 multiply_reduce_fusion
  81.7 0.0 copy-done.2
  81.7 4.5 %fusion.6 = f32[768,768]{0,1:T(8,128)} fusion(bf16[2048,768]{1,0:T(8,128)(2,1)S(1)} %copy-done, f32[2048,768]{0,1:T(8,128)S(1)} %copy-done.6, f32[2048,768]{0,1:T(8,128)S(1)} %get-tuple-element.17, f32[2048]{0:T(1024)S(1)} %get-tuple-element.12, f32[2048]{0:T(1024)S(1)} %get-tuple-element.11), kind=kOutput, calls=%fused_computation.15 | convolution fusion | flops 2423783424 | bytes 18104320 | tf_op jit(solution)/shard_map/dot_general | solution.py:52
  86.2 0.0 all-reduce.2.cloned.1.call-update
  86.2 0.0 reduce-scatter.2.cloned.1.call-start
  86.2 8.7 %multiply_convert_fusion.1 = bf16[1024,768]{1,0:T(8,128)(2,1)} fusion(bf16[2048,1024]{0,1:T(8,128)(2,1)} %copy-done.2, f32[2048,768]{0,1:T(8,128)} %get-tuple-element.14, f32[2048]{0:T(1024)S(1)} %fusion.13), kind=kOutput, calls=%fused_computation.14 | convolution fusion | flops 3225944064 | bytes 12066816 | tf_op jit(solution)/shard_map/dot_general | solution.py:41
  94.9 0.0 copy-start.3
  94.9 0.0 reduce-scatter.2.cloned.1.call-update
  95.0 0.6 log_subtract_fusion
  95.6 253.1 %all-reduce.2.cloned.1.call-done = f32[768,768]{0,1:T(8,128)} async-done(((f32[768,768]{0,1:T(8,128)}), f32[768,768]{0,1:T(8,128)}) %all-reduce.2.cloned.1.call-update) | async-done | bytes 2359312 | tf_op jit(solution)/shard_map/psum | solution.py:55
  348.7 3.0 copy.9
  351.7 76.2 %reduce-scatter.2.cloned.1.call-done = bf16[64,768]{1,0:T(8,128)(2,1)} async-done(((bf16[1024,768]{1,0:T(8,128)(2,1)}), bf16[64,768]{1,0:T(8,128)(2,1)}) %reduce-scatter.2.cloned.1.call-update) | async-done | bytes 98320 | tf_op jit(solution)/shard_map/reduce_scatter | solution.py:39
  427.9 0.0 copy-done.3
  427.9 1.0 fusion.12
  428.9 1.7 add_add_fusion.1
  (5 shorter events, 0.0 us)
Async XLA Ops:
  7.2 13.9 %copy-start = (bf16[2048,768]{1,0:T(8,128)(2,1)S(1)}, bf16[2048,768]{1,0:T(8,128)(2,1)}, u32[]{:S(2)}) copy-start(bf16[2048,768]{1,0:T(8,128)(2,1)} %param.5) | copy-start | bytes 9437188
  7.2 58.3 %all-gather.2.cloned.1.call-start = ((), (), s32[]{:S(2)}) async-start(), calls=%async_computation.1 | async-start | bytes 1671168 | tf_op jit(solution)/shard_map/all_gather | solution.py:23
  10.1 338.6 %all-reduce.2.cloned.1.call-start = ((), (), s32[]{:S(2)}) async-start(), calls=%async_computation.3 | async-start | bytes 4718592 | tf_op jit(solution)/shard_map/psum | solution.py:55
  21.1 5.9 %copy-start.4 = (s32[2048]{0:T(1024)S(1)}, s32[2048]{0:T(1024)}, u32[]{:S(2)}) copy-start(s32[2048]{0:T(1024)} %param.9) | copy-start | bytes 24580
  21.1 44.5 %copy-start.1 = (s32[1024]{0:T(1024)S(1)}, s32[1024]{0:T(1024)}, u32[]{:S(2)}) copy-start(s32[1024]{0:T(1024)} %param.8) | copy-start | bytes 12292
  73.7 3.9 copy-start.5
  73.7 3.9 copy-start.6
  77.6 4.1 copy-start.2
  86.2 341.7 %reduce-scatter.2.cloned.1.call-start = ((), (), s32[]{:S(2)}) async-start(), calls=%async_computation.2 | async-start | bytes 1671168 | tf_op jit(solution)/shard_map/reduce_scatter | solution.py:39
  94.9 333.0 %copy-start.3 = (bf16[64,768]{1,0:T(8,128)(2,1)S(1)}, bf16[64,768]{1,0:T(8,128)(2,1)}, u32[]{:S(2)}) copy-start(bf16[64,768]{1,0:T(8,128)(2,1)} %param.7) | copy-start | bytes 294916
Sparse Core Ops, SparseCore 0:
  11.3 54.1 all-gather.1
  86.3 262.3 all-reduce.1
  352.8 75.0 reduce-scatter.1
where the time goes:
time: 437 us
  waiting for transfers between devices  368 us (84%)
  matrix products  31.2 us (7%)
  between operations  13.9 us (3%)
  local copies, waits for them, and re-layouts  13.3 us (3%)
  other arithmetic  10.7 us (2%)
    psum x1, waiting for transfers between devices, on_device(): grad_weight = lax.psum(weight_term, ('grp', 'blk'))  253 us
    reduce_scatter x1, waiting for transfers between devices, on_device(): lax.psum_scatter((lax.dot_general(weights, query_unit, (((0,), (0,)), (()...  76.2 us
    all_gather x1, waiting for transfers between devices, on_device(): panel = lax.all_gather(candidate_direction, 'blk', axis=0, tiled=True)  38.6 us
    gather x1, local copies, waits for them, and re-layouts, on_device(): anchor_lemma_label = jnp.take(attempt_theorem, positive)  10.2 us
  transfers between devices with their start and end apart: 3, of which 3 were waited for; matrix products, arithmetic and copies ran while one was open for 7% of the time, Pallas kernels for 0%

commit v1 on v0

--- a/solution.py
+++ b/solution.py
@@ -20,7 +20,9 @@
     query_float, query_back = jax.vjp(normalized_rows, proj)
     query_unit = query_float.astype(jnp.bfloat16)
     anchor_lemma_label = jnp.take(attempt_theorem, positive)
-    panel = lax.all_gather(candidate_direction, "blk", axis=0, tiled=True)
+    panel = jnp.concatenate(
+        lax.all_to_all(jnp.stack([candidate_direction] * lax.axis_size("blk")), "blk", 0, 0), axis=0
+    )
     scores = (
         lax.dot_general(
             query_unit, panel, (((1,), (1,)), ((), ())), preferred_element_type=jnp.float32

time: 437 us -> 341 us (0.78)
  waiting for transfers between devices: 368 us -> 261 us
  starting transfers between devices: 0.12 us -> 7.56 us
    reduce_scatter x1, waiting for transfers between devices: 76.2 us -> 0.01 us  [on_device(): lax.psum_scatter((lax.dot_general(weights, query_unit, (((0,), (0,)), (()...]
    all_gather x1 -> x0, waiting for transfers between devices: 38.6 us -> none  [on_device(): panel = lax.all_gather(candidate_direction, 'blk', axis=0, tiled=True)]
    all_to_all x0 -> x1, starting transfers between devices: none -> 7.48 us  [on_device(): lax.all_to_all(jnp.stack([candidate_direction] * lax.axis_size('blk')), '...]
    all_to_all x0 -> x1, waiting for transfers between devices: none -> 6.08 us  [on_device(): lax.all_to_all(jnp.stack([candidate_direction] * lax.axis_size('blk')), '...]
  transfers between devices with their start and end apart: 3 -> 3, of which waited for: 3 -> 2; matrix products, arithmetic and copies ran while one was open for 7% -> 8% of each run, Pallas kernels for 0% -> 0%
where the time goes in v1:
time: 341 us
  waiting for transfers between devices  261 us (77%)
  matrix products  33.8 us (10%)
  between operations  15.6 us (5%)
  local copies, waits for them, and re-layouts  13 us (4%)
  other arithmetic  10.1 us (3%)
  starting transfers between devices  7.56 us (2%)
    psum x1, waiting for transfers between devices, on_device(): grad_weight = lax.psum(weight_term, ('grp', 'blk'))  255 us
    dot_general x1, matrix products, on_device(): lax.dot_general(weights, query_unit, (((0,), (0,)), ((), ())), preferred_...  8.7 us
    gather x1, local copies, waits for them, and re-layouts, on_device(): anchor_lemma_label = jnp.take(attempt_theorem, positive)  8.58 us
    dot_general x1, matrix products, on_device(): lax.dot_general(query_unit, panel, (((1,), (1,)), ((), ())), preferred_el...  8.19 us
    all_to_all x1, starting transfers between devices, on_device(): lax.all_to_all(jnp.stack([candidate_direction] * lax.axis_size('blk')), '...  7.48 us
  transfers between devices with their start and end apart: 3, of which 2 were waited for; matrix products, arithmetic and copies ran while one was open for 8% of the time, Pallas kernels for 0%

profile of v1, /device:TPU:2, one launch (start us, length us, event | category | flops | bytes accessed | tf_op | source)
XLA Modules:
  0.0 341.0 jit_solution(2533566730686601054)
XLA Ops:
  8.0 0.0 copy-start
  8.0 0.0 copy-start.1
  8.0 1.2 fusion.10
  9.2 1.0 fusion.11
  10.2 1.3 stack.2
  11.5 7.5 %all-to-all-start = ((bf16[16,64,768]{2,1,0:T(8,128)(2,1)}), bf16[16,64,768]{2,1,0:T(8,128)(2,1)}, u32[]{:S(2)}, u32[]{:S(2)}) async-start(bf16[16,64,768]{2,1,0:T(8,128)(2,1)} %stack.2), calls=%async_computation | async-start | bytes 3145728 | tf_op jit(solution)/shard_map/all_to_all | solution.py:24
  19.0 0.0 all-reduce.2.cloned.1.call-start
  19.0 0.7 fusion.14
  19.7 0.0 copy-done.1
  19.7 8.6 %gather_fusion = s32[2048]{0:T(1024)S(1)} fusion(s32[1024]{0:T(1024)S(1)} %copy-done.1, s32[2048]{0:T(1024)S(1)} %fusion.14), kind=kCustom, calls=%fused_computation | custom fusion | bytes 24576 | tf_op jit(solution)/shard_map/jit(_take)/gather | solution.py:22
  28.3 0.0 copy-done
  28.3 0.0 copy-start.4
  28.3 5.8 %multiply_reduce_fusion.1 = (f32[2048]{0:T(1024)S(1)}, f32[2048,768]{0,1:T(8,128)}) fusion(bf16[2048,768]{1,0:T(8,128)(2,1)S(1)} %copy-done, bf16[768,768]{1,0:T(8,128)(2,1)} %param.6), kind=kOutput, calls=%fused_computation.10 | convolution fusion | flops 2419062784 | bytes 10625024 | tf_op jit(solution)/shard_map/dot_general | solution.py:19
  34.2 0.0 copy-done.4
  34.2 6.1 %all-to-all-done = bf16[16,64,768]{2,1,0:T(8,128)(2,1)} async-done(((bf16[16,64,768]{2,1,0:T(8,128)(2,1)}), bf16[16,64,768]{2,1,0:T(8,128)(2,1)}, u32[]{:S(2)}, u32[]{:S(2)}) %all-to-all-start) | async-done | bytes 1572896 | tf_op jit(solution)/shard_map/all_to_all | solution.py:24
  40.3 8.2 %fusion = (f32[2048]{0:T(1024)S(1)}, f32[2048]{0:T(1024)S(1)}, f32[2048,1024]{0,1:T(8,128)S(1)}) fusion(s32[2048]{0:T(1024)S(1)} %and_select_fusion, s32[1024]{0:T(1024)S(1)} %copy-done.1, s32[2048]{0:T(1024)S(1)} %copy-done.4, bf16[1024,768]{1,0:T(8,128)(2,1)} %bitcast, f32[2048,768]{0,1:T(8,128)} %get-tuple-element.14, f32[2048]{0:T(1024)S(1)} %fusion.13), kind=kOutput, calls=%fused_computation.6 | convolution fusion | flops 3239047168 | bytes 16297984 | tf_op jit(solution)/shard_map/dot_general | solution.py:27
  48.5 0.0 copy-start.5
  48.5 3.8 %subtract_convert_fusion = bf16[2048,1024]{0,1:T(8,128)(2,1)S(1)} fusion(f32[2048,1024]{0,1:T(8,128)S(1)} %get-tuple-element.15, f32[2048]{0:T(1024)S(1)} %get-tuple-element.9, s32[2048]{0:T(1024)S(1)} %copy-done.4, s32[2048]{0:T(1024)S(1)} %and_select_fusion, s32[1024]{0:T(1024)S(1)} %copy-done.1), kind=kLoop, calls=%fused_computation.2 | loop fusion | flops 16777216 | bytes 12611584 | tf_op jit(solution)/shard_map/convert_element_type | solution.py:39
  52.3 0.0 copy-done.5
  52.3 0.0 copy-start.2
  52.3 6.6 %multiply_reduce_fusion = (f32[2048]{0:T(1024)S(1)}, f32[2048,768]{0,1:T(8,128)S(1)}) fusion(f32[2048,768]{0,1:T(8,128)S(1)} %copy-done.5, bf16[2048,1024]{0,1:T(8,128)(2,1)S(1)} %subtract_convert_fusion, bf16[1024,768]{1,0:T(8,128)(2,1)} %bitcast), kind=kOutput, calls=%fused_computation.8 | convolution fusion | flops 3225942016 | bytes 18358272 | tf_op jit(solution)/shard_map/dot_general | solution.py:40
  59.0 0.0 copy-done.2
  59.0 4.5 %fusion.6 = f32[768,768]{0,1:T(8,128)} fusion(bf16[2048,768]{1,0:T(8,128)(2,1)S(1)} %copy-done, f32[2048,768]{0,1:T(8,128)S(1)} %copy-done.5, f32[2048,768]{0,1:T(8,128)S(1)} %get-tuple-element.17, f32[2048]{0:T(1024)S(1)} %get-tuple-element.12, f32[2048]{0:T(1024)S(1)} %get-tuple-element.11), kind=kOutput, calls=%fused_computation.15 | convolution fusion | flops 2423783424 | bytes 18104320 | tf_op jit(solution)/shard_map/dot_general | solution.py:54
  63.5 0.0 all-reduce.2.cloned.1.call-update
  63.5 0.0 reduce-scatter.2.cloned.1.call-start
  63.5 8.7 %multiply_convert_fusion.1 = bf16[1024,768]{1,0:T(8,128)(2,1)} fusion(bf16[2048,1024]{0,1:T(8,128)(2,1)} %copy-done.2, f32[2048,768]{0,1:T(8,128)} %get-tuple-element.14, f32[2048]{0:T(1024)S(1)} %fusion.13), kind=kOutput, calls=%fused_computation.14 | convolution fusion | flops 3225944064 | bytes 12066816 | tf_op jit(solution)/shard_map/dot_general | solution.py:43
  72.2 0.0 copy-start.3
  72.2 0.0 reduce-scatter.2.cloned.1.call-update
  72.3 0.6 log_subtract_fusion
  72.9 254.9 %all-reduce.2.cloned.1.call-done = f32[768,768]{0,1:T(8,128)} async-done(((f32[768,768]{0,1:T(8,128)}), f32[768,768]{0,1:T(8,128)}) %all-reduce.2.cloned.1.call-update) | async-done | bytes 2359312 | tf_op jit(solution)/shard_map/psum | solution.py:57
  327.8 3.0 copy.9
  330.8 0.0 reduce-scatter.2.cloned.1.call-done
  330.8 0.0 copy-done.3
  330.8 1.0 fusion.12
  331.9 1.7 add_add_fusion.1
  (5 shorter events, 0.0 us)
Async XLA Ops:
  8.0 20.3 %copy-start = (bf16[2048,768]{1,0:T(8,128)(2,1)S(1)}, bf16[2048,768]{1,0:T(8,128)(2,1)}, u32[]{:S(2)}) copy-start(bf16[2048,768]{1,0:T(8,128)(2,1)} %param.5) | copy-start | bytes 9437188
  8.0 11.7 %copy-start.1 = (s32[1024]{0:T(1024)S(1)}, s32[1024]{0:T(1024)}, u32[]{:S(2)}) copy-start(s32[1024]{0:T(1024)} %param.8) | copy-start | bytes 12292
  11.5 28.8 %all-to-all-start = ((bf16[16,64,768]{2,1,0:T(8,128)(2,1)}), bf16[16,64,768]{2,1,0:T(8,128)(2,1)}, u32[]{:S(2)}, u32[]{:S(2)}) async-start(bf16[16,64,768]{2,1,0:T(8,128)(2,1)} %stack.2), calls=%async_computation | async-start | bytes 3145728 | tf_op jit(solution)/shard_map/all_to_all | solution.py:24
  19.0 308.8 %all-reduce.2.cloned.1.call-start = ((), (), s32[]{:S(2)}) async-start(), calls=%async_computation.3 | async-start | bytes 4718592 | tf_op jit(solution)/shard_map/psum | solution.py:57
  28.3 5.9 %copy-start.4 = (s32[2048]{0:T(1024)S(1)}, s32[2048]{0:T(1024)}, u32[]{:S(2)}) copy-start(s32[2048]{0:T(1024)} %param.9) | copy-start | bytes 24580
  48.5 3.9 %copy-start.5 = (f32[2048,768]{0,1:T(8,128)S(1)}, f32[2048,768]{0,1:T(8,128)}, u32[]{:S(2)}) copy-start(f32[2048,768]{0,1:T(8,128)} %get-tuple-element.14) | copy-start | bytes 18874372
  52.3 6.6 %copy-start.2 = (bf16[2048,1024]{0,1:T(8,128)(2,1)}, bf16[2048,1024]{0,1:T(8,128)(2,1)S(1)}, u32[]{:S(2)}) copy-start(bf16[2048,1024]{0,1:T(8,128)(2,1)S(1)} %subtract_convert_fusion) | copy-start | bytes 12582916
  63.5 267.3 %reduce-scatter.2.cloned.1.call-start = ((), (), s32[]{:S(2)}) async-start(), calls=%async_computation.2 | async-start | bytes 1671168 | tf_op jit(solution)/shard_map/reduce_scatter | solution.py:41
  72.2 258.6 %copy-start.3 = (bf16[64,768]{1,0:T(8,128)(2,1)S(1)}, bf16[64,768]{1,0:T(8,128)(2,1)}, u32[]{:S(2)}) copy-start(bf16[64,768]{1,0:T(8,128)(2,1)} %param.7) | copy-start | bytes 294916
Sparse Core Ops, SparseCore 0:
  63.6 264.1 all-reduce.1
Sparse Core Ops, SparseCore 1:
  72.4 77.1 reduce-scatter.1
